TPU v7x, 32 devices: a whole 2x2x4 slice. The times are simulated.
32 devices in a mesh: row: 8 (over z, y), col: 4 (over x, core).
Axes of the slice: x: 2, y: 2, z: 4, core: 2. Of those that a mesh axis runs over, the one named last changes fastest.
Arguments:
- head_deflections: float32 [256, 3, 2, 1024], P('row', None, None, 'col'), may hold values from -6 to 6
- diag_inverse: float32 [2, 1024, 1024], P(None, None, 'col'), may hold values from -1 to 2, as said below
- coupling: float32 [1024, 1024], P(None, 'col'), may hold values from -0.1875 to 0.1875
- panel_factor: float32 [8192, 2, 1024], P('row', None, 'col'), may hold values from -0.125 to 0.125
- trailing: float32 [256, 3, 8192], P('col', None, 'row'), may hold values from -6 to 6
Outputs:
- solved: float32 [256, 3, 2, 1024], P('row', None, None, 'col')
- rest: float32 [256, 3, 8192], P('col', None, 'row')
Inputs may be any that keep to these rules, and one draw needn't show every extreme that they name: Each diag_inverse[p] is lower triangular with a positive diagonal.
All inputs are finite; a program needn't handle non-finite values.
Results may differ from a plain program's by a relative error of at most 0.00007.
Values sent between devices are 32-bit elements; how exact they have to be, the bound alone decides.
No kernel may reach another device: no remote copies, remote signals or barrier semaphores. Data moves between devices by JAX's collectives and lax.ppermute only.
A program may use at most 64 MiB of HBM per device.

v0:
```python
import jax
import jax.numpy as jnp
from jax import lax
from jax.sharding import PartitionSpec as P


def apply_cols(matrix, vectors):
    return lax.dot_general(
        vectors,
        matrix,
        (((2,), (1,)), ((), ())),
        precision=lax.Precision.HIGHEST,
        preferred_element_type=jnp.float32,
    )


def solve_first(block_rhs, diag_inverse):
    return lax.psum_scatter(
        apply_cols(diag_inverse[0], block_rhs), "col", scatter_dimension=2, tiled=True
    )


def solve_second(block_rhs, first_solved, diag_inverse, coupling):
    moved = lax.psum_scatter(
        apply_cols(coupling, first_solved), "col", scatter_dimension=2, tiled=True
    )
    carried = block_rhs - moved
    return lax.psum_scatter(
        apply_cols(diag_inverse[1], carried), "col", scatter_dimension=2, tiled=True
    )


def share_steps(solved_own):
    return lax.all_gather(solved_own, "row", axis=0, tiled=True)


def panel_terms(solved_all, factor):
    return lax.dot_general(
        solved_all,
        factor,
        (((2,), (1,)), ((), ())),
        precision=lax.Precision.HIGHEST,
        preferred_element_type=jnp.float32,
    )


def both_terms(first_all, second_all, panel_factor):
    first_part = panel_terms(first_all, panel_factor[:, 0, :])
    return first_part + panel_terms(second_all, panel_factor[:, 1, :])


def body(head_deflections, diag_inverse, coupling, panel_factor, trailing):
    first_own = solve_first(head_deflections[:, :, 0, :], diag_inverse)
    first_all = share_steps(first_own)
    second_own = solve_second(head_deflections[:, :, 1, :], first_own, diag_inverse, coupling)
    second_all = share_steps(second_own)
    summed = lax.psum_scatter(
        both_terms(first_all, second_all, panel_factor), "col", scatter_dimension=0, tiled=True
    )
    rest = trailing - summed
    solved = jnp.stack([first_own, second_own], axis=2)
    return (solved, rest)


def solution(mesh):
    placed = (
        P("row", None, None, "col"),
        P(None, None, "col"),
        P(None, "col"),
        P("row", None, "col"),
        P("col", None, "row"),
    )
    return jax.shard_map(
        body,
        mesh=mesh,
        in_specs=placed,
        out_specs=(P("row", None, None, "col"), P("col", None, "row")),
        check_vma=False,
    )
```

profile of v0, /device:TPU:0, one launch (start us, length us, event | category | flops | bytes accessed | tf_op | source)
XLA Modules:
  0.0 187.3 jit_solution(2642508243679747117)
XLA Ops:
  7.2 0.0 copy-start
  7.2 0.0 reduce-scatter.5.cloned.1.call-start
  7.2 1.3 fusion.12
  8.6 3.1 %fusion.5 = f32[32,3,1024]{2,0,1:T(8,128)} fusion(f32[2,1024,256]{2,1,0:T(8,128)} %param.6, f32[32,3,1,256]{3,2,1,0:T(1,128)S(1)} %get-tuple-element.9), kind=kOutput, calls=%fused_computation.8 | convolution fusion | flops 301989888 | bytes 1540096 | tf_op jit(solution)/shard_map/dot_general | solution.py:8
  11.7 0.0 reduce-scatter.5.cloned.1.call-update
  11.7 0.0 reduce-scatter.7.cloned.1.call-start
  11.8 23.7 %reduce-scatter.5.cloned.1.call-done = f32[32,3,256]{2,0,1:T(8,128)} async-done(((f32[32,3,1024]{2,0,1:T(8,128)}), f32[32,3,256]{2,0,1:T(8,128)}) %reduce-scatter.5.cloned.1.call-update) | async-done | bytes 98320 | tf_op jit(solution)/shard_map/reduce_scatter | solution.py:18
  35.4 2.8 %fusion.3 = f32[32,3,1024]{2,0,1:T(8,128)} fusion(f32[32,3,256]{2,0,1:T(8,128)} %reduce-scatter.5.cloned.1.call-done, f32[1024,256]{1,0:T(8,128)S(1)} %copy-done), kind=kOutput, calls=%fused_computation.6 | convolution fusion | flops 301989888 | bytes 1540096 | tf_op jit(solution)/shard_map/dot_general | solution.py:8
  38.2 0.0 reduce-scatter.7.cloned.1.call-update
  38.2 0.0 reduce-scatter.9.cloned.1.call-start
  38.3 21.1 %reduce-scatter.7.cloned.1.call-done = f32[32,3,256]{2,0,1:T(8,128)} async-done(((f32[32,3,1024]{2,0,1:T(8,128)}), f32[32,3,256]{2,0,1:T(8,128)}) %reduce-scatter.7.cloned.1.call-update) | async-done | bytes 98320 | tf_op jit(solution)/shard_map/reduce_scatter | solution.py:24
  59.3 2.8 %fusion.1 = f32[32,3,1024]{2,0,1:T(8,128)} fusion(f32[2,1024,256]{2,1,0:T(8,128)S(1)} %copy-done.1, f32[32,3,256]{2,0,1:T(8,128)} %reduce-scatter.7.cloned.1.call-done, f32[32,3,1,256]{3,2,1,0:T(1,128)S(1)} %get-tuple-element.8), kind=kOutput, calls=%fused_computation.4 | convolution fusion | flops 302014464 | bytes 1638400 | tf_op jit(solution)/shard_map/dot_general | solution.py:8
  62.1 0.0 reduce-scatter.9.cloned.1.call-update
  62.2 0.0 reduce-scatter.11.cloned.1.call-start
  62.2 4.0 %fusion.11 = (f32[1024,1,256]{2,1,0:T(1,128)S(1)}, f32[1024,1,256]{2,1,0:T(1,128)S(1)}) fusion(f32[1024,2,256]{2,1,0:T(2,128)} %param.8), kind=kLoop, calls=%fused_computation.16 | loop fusion | bytes 4194304 | tf_op jit(solution)/shard_map/slice | solution.py:49
  66.2 32.2 %all_gather.6 = f32[256,3,256]{2,0,1:T(8,128)S(1)} all-gather(f32[32,3,256]{2,0,1:T(8,128)S(1)} %copy-done.2), channel_id=1, replica_groups=mesh['row'=8,'col'=4] {'row'}, dimensions={0}, use_global_device_ids=true | all-gather | bytes 884736 | tf_op jit(solution)/shard_map/all_gather | solution.py:34
  98.4 4.3 %fusion = f32[256,3,1024]{2,0,1:T(8,128)} fusion(f32[256,3,256]{2,0,1:T(8,128)S(1)} %all_gather.6, f32[1024,1,256]{2,1,0:T(1,128)S(1)} %get-tuple-element.7), kind=kOutput, calls=%fused_computation.3 | convolution fusion | flops 2415919104 | bytes 4980736 | tf_op jit(solution)/shard_map/dot_general | solution.py:38
  102.7 31.9 %all_gather.7 = f32[256,3,256]{2,0,1:T(8,128)S(1)} all-gather(f32[32,3,256]{2,0,1:T(8,128)} %reduce-scatter.9.cloned.1.call-done), channel_id=1, replica_groups=mesh['row'=8,'col'=4] {'row'}, dimensions={0}, use_global_device_ids=true | all-gather | bytes 884736 | tf_op jit(solution)/shard_map/all_gather | solution.py:34
  134.6 5.7 %convolution_add_fusion = f32[256,3,1024]{2,0,1:T(8,128)} fusion(f32[256,3,1024]{2,0,1:T(8,128)} %fusion, f32[256,3,256]{2,0,1:T(8,128)S(1)} %all_gather.7, f32[1024,1,256]{2,1,0:T(1,128)S(1)} %get-tuple-element.6), kind=kOutput, calls=%fused_computation | convolution fusion | flops 2416705536 | bytes 8126464 | tf_op jit(solution)/shard_map/dot_general | solution.py:38
  140.3 0.0 reduce-scatter.11.cloned.1.call-update
  140.3 0.9 copy-done.4
  141.2 0.8 copy.16
  142.0 36.6 %reduce-scatter.11.cloned.1.call-done = f32[64,3,1024]{2,0,1:T(8,128)} async-done(((f32[256,3,1024]{2,0,1:T(8,128)}), f32[64,3,1024]{2,0,1:T(8,128)}) %reduce-scatter.11.cloned.1.call-update) | async-done | bytes 786448 | tf_op jit(solution)/shard_map/reduce_scatter | solution.py:57
  178.6 2.1 %sub.7 = f32[64,3,1024]{2,0,1:T(8,128)} subtract(f32[64,3,1024]{2,0,1:T(8,128)S(1)} %copy-done.3, f32[64,3,1024]{2,0,1:T(8,128)} %reduce-scatter.11.cloned.1.call-done) | non-fusion elementwise | flops 196608 | bytes 2359296 | tf_op jit(solution)/shard_map/sub | solution.py:60
  (10 shorter events, 0.0 us)
Async XLA Ops:
  7.2 28.3 %copy-start = (f32[1024,256]{1,0:T(8,128)S(1)}, f32[1024,256]{1,0:T(8,128)}, u32[]{:S(2)}) copy-start(f32[1024,256]{1,0:T(8,128)} %param.7) | copy-start | bytes 3145732
  7.2 52.2 %copy-start.1 = (f32[2,1024,256]{2,1,0:T(8,128)S(1)}, f32[2,1024,256]{2,1,0:T(8,128)}, u32[]{:S(2)}) copy-start(f32[2,1024,256]{2,1,0:T(8,128)} %param.6) | copy-start | bytes 6291460
  7.2 28.2 %reduce-scatter.5.cloned.1.call-start = ((), (), s32[]{:S(2)}) async-start(), calls=%async_computation.4 | async-start | bytes 491520 | tf_op jit(solution)/shard_map/reduce_scatter | solution.py:18
  11.7 47.6 %reduce-scatter.7.cloned.1.call-start = ((), (), s32[]{:S(2)}) async-start(), calls=%async_computation.5 | async-start | bytes 491520 | tf_op jit(solution)/shard_map/reduce_scatter | solution.py:24
  38.2 64.5 %reduce-scatter.9.cloned.1.call-start = ((), (), s32[]{:S(2)}) async-start(), calls=%async_computation.6 | async-start | bytes 491520 | tf_op jit(solution)/shard_map/reduce_scatter | solution.py:28
  62.1 4.1 %copy-start.2 = (f32[32,3,256]{2,0,1:T(8,128)S(1)}, f32[32,3,256]{2,0,1:T(8,128)}, u32[]{:S(2)}) copy-start(f32[32,3,256]{2,0,1:T(8,128)} %reduce-scatter.5.cloned.1.call-done) | copy-start | bytes 294916
  62.2 116.5 %reduce-scatter.11.cloned.1.call-start = ((), (), s32[]{:S(2)}) async-start(), calls=%async_computation.7 | async-start | bytes 3932160 | tf_op jit(solution)/shard_map/reduce_scatter | solution.py:57
  140.3 0.9 copy-start.4
  140.3 38.4 %copy-start.3 = (f32[64,3,1024]{2,0,1:T(8,128)S(1)}, f32[64,3,1024]{2,0,1:T(8,128)}, u32[]{:S(2)}) copy-start(f32[64,3,1024]{2,0,1:T(8,128)} %param.9) | copy-start | bytes 2359300
Sparse Core Ops, SparseCore 0:
  11.8 23.5 reduce-scatter.4
  38.5 20.8 reduce-scatter.6
  62.4 20.8 reduce-scatter.8
  140.4 38.1 reduce-scatter.10
where the time goes:
time: 188 us; the launch traced here: 187 us
  waiting for transfers between devices  81.4 us (43%)
  blocking collectives  64 us (34%)
  matrix products  18.7 us (10%)
  between operations  13.8 us (7%)
  local copies, waits for them, and re-layouts  7.09 us (4%)
  other arithmetic  2.12 us (1%)
    all_gather x2, blocking collectives, share_steps(): return lax.all_gather(solved_own, 'row', axis=0, tiled=True)  64 us
    reduce_scatter x1, waiting for transfers between devices, body(): lax.psum_scatter(both_terms(first_all, second_all, panel_factor), 'col',...  36.6 us
    reduce_scatter x1, waiting for transfers between devices, solve_first(): lax.psum_scatter(apply_cols(diag_inverse[0], block_rhs), 'col', scatter_d...  23.7 us
    reduce_scatter x1, waiting for transfers between devices, solve_second(): lax.psum_scatter(apply_cols(coupling, first_solved), 'col', scatter_dimen...  21.1 us
    dot_general x2, matrix products, panel_terms(): lax.dot_general(solved_all, factor, (((2,), (1,)), ((), ())), precision=l...  10 us
    dot_general x3, matrix products, apply_cols(): lax.dot_general(vectors, matrix, (((2,), (1,)), ((), ())), precision=lax....  8.65 us
    slice x1, local copies, waits for them, and re-layouts, both_terms(): return first_part + panel_terms(second_all, panel_factor[:, 1, :])  4.02 us
  transfers between devices with their start and end apart: 4, of which 3 were waited for; matrix products, arithmetic and copies ran while one was open for 5% of the time, Pallas kernels for 0%

commit v1 on v0

v1 whole, which is shorter than its diff:
```python
import jax
import jax.numpy as jnp
from jax import lax
from jax.sharding import PartitionSpec as P

SOLVE = lax.Precision.HIGHEST
UPDATE = lax.Precision.HIGH


def apply_rows(vectors, matrix, precision):
    return lax.dot_general(
        vectors,
        matrix,
        (((1,), (1,)), ((), ())),
        precision=precision,
        preferred_element_type=jnp.float32,
    )


def apply_pair(vectors, own, other, precision):
    width = own.shape[1]
    near = apply_rows(vectors[:, :width], own, precision)
    return near + apply_rows(vectors[:, width:], other, precision)


def make_body(n_row, n_col):
    n_x = n_col // 2
    n_y = n_x
    n_z = n_row // n_y
    assert n_z == 2 * n_x and n_y * n_z == n_row

    def col_permute(value, pairs):
        return lax.ppermute(value, "col", pairs)

    def core_swap(value):
        return col_permute(value, [(c, c ^ 1) for c in range(n_col)])

    def x_shift(value, step, up_only=False):
        pairs = []
        for x in range(n_x):
            if x + step < n_x or not up_only:
                pairs += [(2 * x + k, 2 * ((x + step) % n_x) + k) for k in range(2)]
        return col_permute(value, pairs)

    def z_round(value, even):
        first, second = even, even ^ 1
        pairs = []
        for z in range(n_z):
            for y in range(n_y):
                for c in range(n_col):
                    x, k = divmod(c, 2)
                    step = first if k == z % 2 else second
                    to = ((z + step) % n_z * n_y + y) * n_col + 2 * x + z % 2
                    pairs.append(((z * n_y + y) * n_col + c, to))
        pairs = [(a, b) for a, b in pairs if a != b]
        return lax.ppermute(value, ("row", "col"), pairs)

    def y_shift(value, step):
        pairs = []
        for z in range(n_z):
            for y in range(n_y):
                pairs.append((z * n_y + y, z * n_y + (y + step) % n_y))
        return lax.ppermute(value, "row", pairs)

    def body(head, diag, coupling, factor, trailing):
        steps, comps, _, quarter = head.shape
        unknowns = diag.shape[1]
        rows = factor.shape[0]
        block = unknowns // n_x
        half = steps // 2
        vecs = half * comps
        col = lax.axis_index("col")
        x, k = col // 2, col % 2
        z = lax.axis_index("row") // n_y
        y = lax.axis_index("row") % n_y
        upper = k == 1

        def turn(value):
            return jnp.where(upper, jnp.roll(value, quarter, axis=-1), value)

        def aim(value):
            return jnp.where(k == z % 2, value, jnp.roll(value, quarter, axis=-1))

        def x_block(value, index):
            return lax.dynamic_slice_in_dim(value, index * block, block, axis=1)

        def x_sum(value, up_only):
            total = x_block(value, x)
            for step in range(1, n_x):
                to = x + step
                to = jnp.minimum(to, n_x - 1) if up_only else to % n_x
                total = total + x_shift(x_block(value, to), step, up_only)
            return total

        split = head.reshape(2, half, comps, 2, quarter).transpose(3, 0, 2, 1, 4)
        split = jnp.where(upper, split[:, ::-1], split)
        split = split.reshape(2, 2 * vecs, quarter)

        coupling_other = core_swap(coupling)
        second_other = core_swap(diag[1])
        factor0, factor1 = factor[:, 0, :], factor[:, 1, :]
        factor0_other = core_swap(factor0)
        factor1_other = core_swap(factor1)

        part = apply_rows(split[0], diag[0], SOLVE)
        part = part[:vecs] + core_swap(part[vecs:])
        first = turn(x_sum(part, True))
        own_rhs = split[1, :vecs]
        rhs = jnp.concatenate([own_rhs, core_swap(split[1, vecs:])], axis=1)

        moved = x_sum(apply_pair(first, coupling, coupling_other, SOLVE), False)
        carried = rhs - turn(moved)
        part = apply_pair(carried, diag[1], second_other, SOLVE)
        second = turn(x_sum(part, True))

        def z_gather(value):
            got = []
            match = k == z % 2
            for even in range(0, n_z, 2):
                one = z_round(value, even)
                two = z_round(value, even + 1)
                if even == 0:
                    one = jnp.where(match, value, one)
                got.append((one, two))
            near = jnp.stack([g[0] for g in got])
            far = jnp.stack([g[1] for g in got])
            return near, far

        zq = (z - jnp.where(k == z % 2, 0, 1)) // 2

        def by_target(stack):
            return [
                lax.dynamic_index_in_dim(stack, (zq - x - t) % n_x, 0, keepdims=False)
                for t in range(n_x)
            ]

        first_near, first_far = z_gather(aim(first))
        second_near, second_far = z_gather(aim(second))

        firsts, seconds = [], []
        for u in range(n_y):
            move = (lambda v, u=u: v) if u == 0 else (lambda v, u=u: y_shift(v, u))
            firsts.append((move(first_near), move(first_far)))
            seconds.append((move(second_near), move(second_far)))

        rest = trailing
        for u in range(n_y):
            for kind in range(2):
                a = by_target(firsts[u][kind])
                b = by_target(seconds[u][kind])
                parts = [
                    apply_pair(p, factor0, factor0_other, UPDATE)
                    + apply_pair(q, factor1, factor1_other, UPDATE)
                    for p, q in zip(a, b)
                ]
                total = parts[0]
                for t in range(1, n_x):
                    total = total + x_shift(parts[t], t)
                total = total.reshape(comps, half, rows).transpose(1, 0, 2)
                at_half = z % 2 if kind == 0 else 1 - z % 2
                at = ((y - u) % n_y) * steps + at_half * half
                old = lax.dynamic_slice_in_dim(trailing, at, half, axis=0)
                rest = lax.dynamic_update_slice_in_dim(rest, old - total, at, axis=0)

        both = jnp.stack([first, second])
        mine = both[:, :, :quarter]
        theirs = core_swap(both[:, :, quarter:])
        lower = jnp.where(upper, theirs, mine)
        higher = jnp.where(upper, mine, theirs)
        solved = jnp.stack([lower, higher]).reshape(2, 2, comps, half, quarter)
        solved = solved.transpose(0, 3, 2, 1, 4).reshape(steps, comps, 2, quarter)
        return solved, rest

    return body


def solution(mesh):
    placed = (
        P("row", None, None, "col"),
        P(None, None, "col"),
        P(None, "col"),
        P("row", None, "col"),
        P("col", None, "row"),
    )
    return jax.shard_map(
        make_body(mesh.shape["row"], mesh.shape["col"]),
        mesh=mesh,
        in_specs=placed,
        out_specs=(P("row", None, None, "col"), P("col", None, "row")),
        check_vma=False,
    )
```

time: 188 us -> 106 us (0.56)
  blocking collectives: 64 us -> 0 us
  waiting for transfers between devices: 81.4 us -> 25.1 us
  starting transfers between devices: 0.16 us -> 36.5 us
  between operations: 13.8 us -> 1.39 us
  matrix products: 18.7 us -> 28.1 us
  local copies, waits for them, and re-layouts: 7.09 us -> 11.8 us
    reduce_scatter x4 -> x0, waiting for transfers between devices: 81.4 us -> none  [the longest x1 36.6 us: body(): lax.psum_scatter(both_terms(first_all, second_all, panel_factor), 'col',...]
    all_gather x2 -> x0, blocking collectives: 64 us -> none  [share_steps(): return lax.all_gather(solved_own, 'row', axis=0, tiled=True)]
    ppermute x0 -> x26, starting transfers between devices: none -> 36.5 us  [the longest x14 17.3 us: col_permute(): return lax.ppermute(value, 'col', pairs)]
    ppermute x0 -> x26, waiting for transfers between devices: none -> 25.1 us  [the longest x8 10.7 us: z_round(): return lax.ppermute(value, ('row', 'col'), pairs)]
    dot_general x5 -> x37, matrix products: 18.7 us -> 28.1 us  [apply_rows(): lax.dot_general(vectors, matrix, (((1,), (1,)), ((), ())), precision=prec...]
    squeeze x0 -> x5, local copies, waits for them, and re-layouts: none -> 3.78 us  [the longest x1 2.26 us: body(): part = apply_pair(carried, diag[1], second_other, SOLVE)]
    slice x2 -> x8, local copies, waits for them, and re-layouts: 5.37 us -> 2.36 us  [the longest x1 1.62 us: body(): factor0, factor1 = (factor[:, 0, :], factor[:, 1, :])]
    sub x1, other arithmetic: 2.1 us -> 0.03 us  [body(): carried = rhs - turn(moved)]
  transfers between devices with their start and end apart: 4 -> 26, of which waited for: 3 -> 11; matrix products, arithmetic and copies ran while one was open for 5% -> 34% of each run, Pallas kernels for 0% -> 0%
where the time goes in v1:
time: 106 us; the launch traced here: 105 us
  starting transfers between devices  36.5 us (34%)
  matrix products  28.1 us (27%)
  waiting for transfers between devices  25.1 us (24%)
  local copies, waits for them, and re-layouts  11.8 us (11%)
  other arithmetic  2.46 us (2%)
  between operations  1.39 us (1%)
    dot_general x37, matrix products, apply_rows(): lax.dot_general(vectors, matrix, (((1,), (1,)), ((), ())), precision=prec...  28.1 us
    ppermute x14, starting transfers between devices, col_permute(): return lax.ppermute(value, 'col', pairs)  17.3 us
    ppermute x8, starting transfers between devices, z_round(): return lax.ppermute(value, ('row', 'col'), pairs)  13.9 us
    ppermute x8, waiting for transfers between devices, z_round(): return lax.ppermute(value, ('row', 'col'), pairs)  10.7 us
    ppermute x14, waiting for transfers between devices, col_permute(): return lax.ppermute(value, 'col', pairs)  7.69 us
    ppermute x4, waiting for transfers between devices, y_shift(): return lax.ppermute(value, 'row', pairs)  6.67 us
    ppermute x4, starting transfers between devices, y_shift(): return lax.ppermute(value, 'row', pairs)  5.26 us
    unnamed x20, local copies, waits for them, and re-layouts  3.68 us
  transfers between devices with their start and end apart: 26, of which 11 were waited for; matrix products, arithmetic and copies ran while one was open for 34% of the time, Pallas kernels for 0%

profile of v1, /device:TPU:0, one launch (start us, length us, event | category | flops | bytes accessed | tf_op | source)
XLA Modules:
  0.0 105.3 jit_solution(10864704282930981487)
XLA Ops:
  1.8 2.4 %fusion.12 = f32[96,1024]{1,0:T(8,128)S(1)} fusion(f32[96,256]{1,0:T(8,128)S(1)} %bitcast.130, f32[2,1024,256]{2,1,0:T(8,128)} %param.6), kind=kOutput, calls=%fused_computation.32 | convolution fusion | flops 301989888 | bytes 1540096 | tf_op jit(solution)/shard_map/dot_general | solution.py:11
  5.4 1.6 %fusion.86 = (f32[1024,1,256]{2,1,0:T(1,128)S(1)}, f32[1024,1,256]{2,1,0:T(1,128)S(1)}) fusion(f32[1024,2,256]{2,1,0:T(2,128)S(1)} %copy-done.4), kind=kLoop, calls=%fused_computation.164 | loop fusion | bytes 4194304 | tf_op jit(solution)/shard_map/slice | solution.py:101
  10.3 4.4 %collective-permute-start.1 = (f32[48,512]{1,0:T(8,128)S(1)}, f32[48,512]{1,0:T(8,128)S(1)}, u32[]{:S(2)}, u32[]{:S(2)}) collective-permute-start(f32[48,512]{1,0:T(8,128)S(1)} %constant_dynamic-slice_fusion.2), channel_id=1, source_target_pairs={{0,2},{1,3},{4,6},{5,7},{8,10},{9,11},{12,14},{13,15},{16,18},{17,... | collective-permute-start | bytes 294920 | tf_op jit(solution)/shard_map/ppermute | solution.py:33
  19.0 2.3 %slice_bitcast_fusion = f32[1024,256]{1,0:T(8,128)} fusion(f32[2,1024,256]{2,1,0:T(8,128)} %param.6), kind=kLoop, calls=%fused_computation.34 | loop fusion | bytes 2097152 | tf_op jit(solution)/shard_map/squeeze | solution.py:113
  22.3 3.6 %collective-permute-start.15 = (f32[48,512]{1,0:T(8,128)S(1)}, f32[48,512]{1,0:T(8,128)S(1)}, u32[]{:S(2)}, u32[]{:S(2)}) collective-permute-start(f32[48,512]{1,0:T(8,128)S(1)} %maximum_select_fusion.3), channel_id=1, source_target_pairs={{0,8},{1,0},{2,10},{3,2},{4,12},{5,4},{6,14},{7,6},{8,9},{9,17},{1... | collective-permute-start | bytes 294920 | tf_op jit(solution)/shard_map/ppermute | solution.py:56
  26.0 1.9 %collective-permute-start.16 = (f32[48,512]{1,0:T(8,128)S(1)}, f32[48,512]{1,0:T(8,128)S(1)}, u32[]{:S(2)}, u32[]{:S(2)}) collective-permute-start(f32[48,512]{1,0:T(8,128)S(1)} %maximum_select_fusion.3), channel_id=1, source_target_pairs={{0,24},{1,16},{2,26},{3,18},{4,28},{5,20},{6,30},{7,22},{8,25},{9,... | collective-permute-start | bytes 294920 | tf_op jit(solution)/shard_map/ppermute | solution.py:56
  28.2 1.8 %collective-permute-start.9 = (f32[48,512]{1,0:T(8,128)S(1)}, f32[48,512]{1,0:T(8,128)S(1)}, u32[]{:S(2)}, u32[]{:S(2)}) collective-permute-start(f32[48,512]{1,0:T(8,128)S(1)} %maximum_select_fusion.3), channel_id=1, source_target_pairs={{0,16},{1,24},{2,18},{3,26},{4,20},{5,28},{6,22},{7,30},{8,1},{9,2... | collective-permute-start | bytes 294920 | tf_op jit(solution)/shard_map/ppermute | solution.py:56
  29.9 5.2 %collective-permute-done.16 = f32[48,512]{1,0:T(8,128)S(1)} collective-permute-done((f32[48,512]{1,0:T(8,128)S(1)}, f32[48,512]{1,0:T(8,128)S(1)}, u32[]{:S(2)}, u32[]{:S(2)}) %collective-permute-start.16) | collective-permute-done | bytes 98336 | tf_op jit(solution)/shard_map/ppermute | solution.py:56
  36.3 1.6 %collective-permute-start.23 = (f32[2,48,512]{2,1,0:T(8,128)S(1)}, f32[2,48,512]{2,1,0:T(8,128)S(1)}, u32[]{:S(2)}, u32[]{:S(2)}) collective-permute-start(f32[2,48,512]{2,1,0:T(8,128)S(1)} %pad_maximum_fusion.2), channel_id=1, source_target_pairs={{0,4},{4,0},{8,12},{12,8},{16,20},{20,16},{24,28},{28,24},{1,5},{5... | collective-permute-start | bytes 589832 | tf_op jit(solution)/shard_map/ppermute | solution.py:63
  40.8 3.3 %collective-permute-done.23 = f32[2,48,512]{2,1,0:T(8,128)S(1)} collective-permute-done((f32[2,48,512]{2,1,0:T(8,128)S(1)}, f32[2,48,512]{2,1,0:T(8,128)S(1)}, u32[]{:S(2)}, u32[]{:S(2)}) %collective-permute-start.23) | collective-permute-done | bytes 196640 | tf_op jit(solution)/shard_map/ppermute | solution.py:63
  44.2 3.3 %collective-permute-done.20 = f32[2,48,512]{2,1,0:T(8,128)S(1)} collective-permute-done((f32[2,48,512]{2,1,0:T(8,128)S(1)}, f32[2,48,512]{2,1,0:T(8,128)S(1)}, u32[]{:S(2)}, u32[]{:S(2)}) %collective-permute-start.20) | collective-permute-done | bytes 196640 | tf_op jit(solution)/shard_map/ppermute | solution.py:63
  47.6 2.3 %fusion.83 = f32[48,1024]{1,0:T(8,128)S(1)} fusion(f32[1024,256]{1,0:T(8,128)} %collective-permute-done.3, f32[48,512]{1,0:T(8,128)S(1)} %maximum_select_fusion), kind=kOutput, calls=%fused_computation.161 | convolution fusion | flops 150994944 | bytes 1294336 | tf_op jit(solution)/shard_map/dot_general | solution.py:11
  49.9 2.3 %convolution_add_fusion.17 = f32[48,1024]{1,0:T(8,128)S(1)} fusion(f32[48,1024]{1,0:T(8,128)S(1)} %fusion.83, f32[1024,256]{1,0:T(8,128)} %param.7, f32[48,512]{1,0:T(8,128)S(1)} %maximum_select_fusion), kind=kOutput, calls=%fused_computation.17 | convolution fusion | flops 151044096 | bytes 1490944 | tf_op jit(solution)/shard_map/dot_general | solution.py:11
  52.2 2.5 %collective-permute-start.4 = (f32[48,512]{1,0:T(8,128)S(1)}, f32[48,512]{1,0:T(8,128)S(1)}, u32[]{:S(2)}, u32[]{:S(2)}) collective-permute-start(f32[48,512]{1,0:T(8,128)S(1)} %constant_dynamic-slice_fusion.1), channel_id=1, source_target_pairs={{0,2},{1,3},{2,0},{3,1},{4,6},{5,7},{6,4},{7,5},{8,10},{9,11},{10,... | collective-permute-start | bytes 294920 | tf_op jit(solution)/shard_map/ppermute | solution.py:33
  56.6 1.7 %collective-permute-done.4 = f32[48,512]{1,0:T(8,128)S(1)} collective-permute-done((f32[48,512]{1,0:T(8,128)S(1)}, f32[48,512]{1,0:T(8,128)S(1)}, u32[]{:S(2)}, u32[]{:S(2)}) %collective-permute-start.4) | collective-permute-done | bytes 98336 | tf_op jit(solution)/shard_map/ppermute | solution.py:33
  60.5 3.6 %collective-permute-start.6 = (f32[48,512]{1,0:T(8,128)S(1)}, f32[48,512]{1,0:T(8,128)S(1)}, u32[]{:S(2)}, u32[]{:S(2)}) collective-permute-start(f32[48,512]{1,0:T(8,128)S(1)} %constant_dynamic-slice_fusion), channel_id=1, source_target_pairs={{0,2},{1,3},{4,6},{5,7},{8,10},{9,11},{12,14},{13,15},{16,18},{17,... | collective-permute-start | bytes 294920 | tf_op jit(solution)/shard_map/ppermute | solution.py:33
  64.8 1.6 %collective-permute-done.6 = f32[48,512]{1,0:T(8,128)S(1)} collective-permute-done((f32[48,512]{1,0:T(8,128)S(1)}, f32[48,512]{1,0:T(8,128)S(1)}, u32[]{:S(2)}, u32[]{:S(2)}) %collective-permute-start.6) | collective-permute-done | bytes 98336 | tf_op jit(solution)/shard_map/ppermute | solution.py:33
  67.2 2.9 %collective-permute-start.17 = (f32[48,512]{1,0:T(8,128)S(1)}, f32[48,512]{1,0:T(8,128)S(1)}, u32[]{:S(2)}, u32[]{:S(2)}) collective-permute-start(f32[48,512]{1,0:T(8,128)S(1)} %maximum_select_fusion.4), channel_id=1, source_target_pairs={{0,8},{1,0},{2,10},{3,2},{4,12},{5,4},{6,14},{7,6},{8,9},{9,17},{1... | collective-permute-start | bytes 294920 | tf_op jit(solution)/shard_map/ppermute | solution.py:56
  70.1 2.3 %collective-permute-start.18 = (f32[48,512]{1,0:T(8,128)S(1)}, f32[48,512]{1,0:T(8,128)S(1)}, u32[]{:S(2)}, u32[]{:S(2)}) collective-permute-start(f32[48,512]{1,0:T(8,128)S(1)} %maximum_select_fusion.4), channel_id=1, source_target_pairs={{0,24},{1,16},{2,26},{3,18},{4,28},{5,20},{6,30},{7,22},{8,25},{9,... | collective-permute-start | bytes 294920 | tf_op jit(solution)/shard_map/ppermute | solution.py:56
  74.3 1.6 %collective-permute-start.21 = (f32[2,48,512]{2,1,0:T(8,128)S(1)}, f32[2,48,512]{2,1,0:T(8,128)S(1)}, u32[]{:S(2)}, u32[]{:S(2)}) collective-permute-start(f32[2,48,512]{2,1,0:T(8,128)S(1)} %pad_maximum_fusion.1), channel_id=1, source_target_pairs={{0,4},{4,0},{8,12},{12,8},{16,20},{20,16},{24,28},{28,24},{1,5},{5... | collective-permute-start | bytes 589832 | tf_op jit(solution)/shard_map/ppermute | solution.py:63
  75.9 3.1 %collective-permute-done.18 = f32[48,512]{1,0:T(8,128)S(1)} collective-permute-done((f32[48,512]{1,0:T(8,128)S(1)}, f32[48,512]{1,0:T(8,128)S(1)}, u32[]{:S(2)}, u32[]{:S(2)}) %collective-permute-start.18) | collective-permute-done | bytes 98336 | tf_op jit(solution)/shard_map/ppermute | solution.py:56
  83.2 2.5 %collective-permute-start.19 = (f32[48,1024]{1,0:T(8,128)S(1)}, f32[48,1024]{1,0:T(8,128)S(1)}, u32[]{:S(2)}, u32[]{:S(2)}) collective-permute-start(f32[48,1024]{1,0:T(8,128)S(1)} %fusion.5), channel_id=1, source_target_pairs={{0,2},{1,3},{2,0},{3,1},{4,6},{5,7},{6,4},{7,5},{8,10},{9,11},{10,... | collective-permute-start | bytes 589832 | tf_op jit(solution)/shard_map/ppermute | solution.py:33
  93.3 2.1 %collective-permute-start.25 = (f32[48,1024]{1,0:T(8,128)S(1)}, f32[48,1024]{1,0:T(8,128)S(1)}, u32[]{:S(2)}, u32[]{:S(2)}) collective-permute-start(f32[48,1024]{1,0:T(8,128)S(1)} %fusion.11), channel_id=1, source_target_pairs={{0,2},{1,3},{2,0},{3,1},{4,6},{5,7},{6,4},{7,5},{8,10},{9,11},{10,... | collective-permute-start | bytes 589832 | tf_op jit(solution)/shard_map/ppermute | solution.py:33
  99.8 3.4 %collective-permute-done.22 = f32[48,1024]{1,0:T(8,128)S(1)} collective-permute-done((f32[48,1024]{1,0:T(8,128)S(1)}, f32[48,1024]{1,0:T(8,128)S(1)}, u32[]{:S(2)}, u32[]{:S(2)}) %collective-permute-start.22) | collective-permute-done | bytes 196640 | tf_op jit(solution)/shard_map/ppermute | solution.py:33
  (130 shorter events, 40.6 us)
Async XLA Ops:
  8.1 46.7 %collective-permute-start.10 = (f32[1024,256]{1,0:T(8,128)}, f32[1024,256]{1,0:T(8,128)S(1)}, u32[]{:S(2)}, u32[]{:S(2)}) collective-permute-start(f32[1024,256]{1,0:T(8,128)} %bitcast.117), channel_id=1, source_target_pairs={{0,1},{1,0},{2,3},{3,2},{4,5},{5,4},{6,7},{7,6},{8,9},{9,8},{10,11... | collective-permute-start | bytes 3145736 | tf_op jit(solution)/shard_map/ppermute | solution.py:33
  8.1 39.4 %collective-permute-start.3 = (f32[1024,256]{1,0:T(8,128)}, f32[1024,256]{1,0:T(8,128)}, u32[]{:S(2)}, u32[]{:S(2)}) collective-permute-start(f32[1024,256]{1,0:T(8,128)} %param.7), channel_id=1, source_target_pairs={{0,1},{1,0},{2,3},{3,2},{4,5},{5,4},{6,7},{7,6},{8,9},{9,8},{10,11... | collective-permute-start | bytes 3145736 | tf_op jit(solution)/shard_map/ppermute | solution.py:33
  10.3 7.1 %collective-permute-start.1 = (f32[48,512]{1,0:T(8,128)S(1)}, f32[48,512]{1,0:T(8,128)S(1)}, u32[]{:S(2)}, u32[]{:S(2)}) collective-permute-start(f32[48,512]{1,0:T(8,128)S(1)} %constant_dynamic-slice_fusion.2), channel_id=1, source_target_pairs={{0,2},{1,3},{4,6},{5,7},{8,10},{9,11},{12,14},{13,15},{16,18},{17,... | collective-permute-start | bytes 294920 | tf_op jit(solution)/shard_map/ppermute | solution.py:33
  16.1 42.2 %collective-permute-start.2 = (f32[48,256]{1,0:T(8,128)}, f32[48,256]{1,0:T(8,128)S(1)}, u32[]{:S(2)}, u32[]{:S(2)}) collective-permute-start(f32[48,256]{1,0:T(8,128)} %get-tuple-element.23), channel_id=1, source_target_pairs={{0,1},{1,0},{2,3},{3,2},{4,5},{5,4},{6,7},{7,6},{8,9},{9,8},{10,11... | collective-permute-start | bytes 147464 | tf_op jit(solution)/shard_map/ppermute | solution.py:33
  18.3 7.6 %collective-permute-start.8 = (f32[48,512]{1,0:T(8,128)S(1)}, f32[48,512]{1,0:T(8,128)S(1)}, u32[]{:S(2)}, u32[]{:S(2)}) collective-permute-start(f32[48,512]{1,0:T(8,128)S(1)} %maximum_select_fusion.3), channel_id=1, source_target_pairs={{1,8},{3,10},{5,12},{7,14},{8,17},{10,19},{12,21},{14,23},{17,24},... | collective-permute-start | bytes 294920 | tf_op jit(solution)/shard_map/ppermute | solution.py:56
  22.3 5.9 %collective-permute-start.15 = (f32[48,512]{1,0:T(8,128)S(1)}, f32[48,512]{1,0:T(8,128)S(1)}, u32[]{:S(2)}, u32[]{:S(2)}) collective-permute-start(f32[48,512]{1,0:T(8,128)S(1)} %maximum_select_fusion.3), channel_id=1, source_target_pairs={{0,8},{1,0},{2,10},{3,2},{4,12},{5,4},{6,14},{7,6},{8,9},{9,17},{1... | collective-permute-start | bytes 294920 | tf_op jit(solution)/shard_map/ppermute | solution.py:56
  26.0 9.1 %collective-permute-start.16 = (f32[48,512]{1,0:T(8,128)S(1)}, f32[48,512]{1,0:T(8,128)S(1)}, u32[]{:S(2)}, u32[]{:S(2)}) collective-permute-start(f32[48,512]{1,0:T(8,128)S(1)} %maximum_select_fusion.3), channel_id=1, source_target_pairs={{0,24},{1,16},{2,26},{3,18},{4,28},{5,20},{6,30},{7,22},{8,25},{9,... | collective-permute-start | bytes 294920 | tf_op jit(solution)/shard_map/ppermute | solution.py:56
  28.2 8.0 %collective-permute-start.9 = (f32[48,512]{1,0:T(8,128)S(1)}, f32[48,512]{1,0:T(8,128)S(1)}, u32[]{:S(2)}, u32[]{:S(2)}) collective-permute-start(f32[48,512]{1,0:T(8,128)S(1)} %maximum_select_fusion.3), channel_id=1, source_target_pairs={{0,16},{1,24},{2,18},{3,26},{4,20},{5,28},{6,22},{7,30},{8,1},{9,2... | collective-permute-start | bytes 294920 | tf_op jit(solution)/shard_map/ppermute | solution.py:56
  36.3 7.8 %collective-permute-start.23 = (f32[2,48,512]{2,1,0:T(8,128)S(1)}, f32[2,48,512]{2,1,0:T(8,128)S(1)}, u32[]{:S(2)}, u32[]{:S(2)}) collective-permute-start(f32[2,48,512]{2,1,0:T(8,128)S(1)} %pad_maximum_fusion.2), channel_id=1, source_target_pairs={{0,4},{4,0},{8,12},{12,8},{16,20},{20,16},{24,28},{28,24},{1,5},{5... | collective-permute-start | bytes 589832 | tf_op jit(solution)/shard_map/ppermute | solution.py:63
  37.9 9.6 %collective-permute-start.20 = (f32[2,48,512]{2,1,0:T(8,128)S(1)}, f32[2,48,512]{2,1,0:T(8,128)S(1)}, u32[]{:S(2)}, u32[]{:S(2)}) collective-permute-start(f32[2,48,512]{2,1,0:T(8,128)S(1)} %pad_maximum_fusion), channel_id=1, source_target_pairs={{0,4},{4,0},{8,12},{12,8},{16,20},{20,16},{24,28},{28,24},{1,5},{5... | collective-permute-start | bytes 589832 | tf_op jit(solution)/shard_map/ppermute | solution.py:63
  44.2 14.1 %collective-permute-start.5 = (f32[1024,256]{1,0:T(8,128)S(1)}, f32[1024,256]{1,0:T(8,128)S(1)}, u32[]{:S(2)}, u32[]{:S(2)}) collective-permute-start(f32[1024,256]{1,0:T(8,128)S(1)} %copy-done.5), channel_id=1, source_target_pairs={{0,1},{1,0},{2,3},{3,2},{4,5},{5,4},{6,7},{7,6},{8,9},{9,8},{10,11... | collective-permute-start | bytes 3145736 | tf_op jit(solution)/shard_map/ppermute | solution.py:33
  47.5 34.4 %collective-permute-start.13 = (f32[1024,256]{1,0:T(8,128)S(1)}, f32[1024,256]{1,0:T(8,128)S(1)}, u32[]{:S(2)}, u32[]{:S(2)}) collective-permute-start(f32[1024,256]{1,0:T(8,128)S(1)} %bitcast.123), channel_id=1, source_target_pairs={{0,1},{1,0},{2,3},{3,2},{4,5},{5,4},{6,7},{7,6},{8,9},{9,8},{10,11... | collective-permute-start | bytes 3145736 | tf_op jit(solution)/shard_map/ppermute | solution.py:33
  52.2 6.0 %collective-permute-start.4 = (f32[48,512]{1,0:T(8,128)S(1)}, f32[48,512]{1,0:T(8,128)S(1)}, u32[]{:S(2)}, u32[]{:S(2)}) collective-permute-start(f32[48,512]{1,0:T(8,128)S(1)} %constant_dynamic-slice_fusion.1), channel_id=1, source_target_pairs={{0,2},{1,3},{2,0},{3,1},{4,6},{5,7},{6,4},{7,5},{8,10},{9,11},{10,... | collective-permute-start | bytes 294920 | tf_op jit(solution)/shard_map/ppermute | solution.py:33
  66.5 6.0 %collective-permute-start.11 = (f32[48,512]{1,0:T(8,128)S(1)}, f32[48,512]{1,0:T(8,128)S(1)}, u32[]{:S(2)}, u32[]{:S(2)}) collective-permute-start(f32[48,512]{1,0:T(8,128)S(1)} %maximum_select_fusion.4), channel_id=1, source_target_pairs={{1,8},{3,10},{5,12},{7,14},{8,17},{10,19},{12,21},{14,23},{17,24},... | collective-permute-start | bytes 294920 | tf_op jit(solution)/shard_map/ppermute | solution.py:56
  67.1 7.2 %collective-permute-start.12 = (f32[48,512]{1,0:T(8,128)S(1)}, f32[48,512]{1,0:T(8,128)S(1)}, u32[]{:S(2)}, u32[]{:S(2)}) collective-permute-start(f32[48,512]{1,0:T(8,128)S(1)} %maximum_select_fusion.4), channel_id=1, source_target_pairs={{0,16},{1,24},{2,18},{3,26},{4,20},{5,28},{6,22},{7,30},{8,1},{9,2... | collective-permute-start | bytes 294920 | tf_op jit(solution)/shard_map/ppermute | solution.py:56
  67.2 8.7 %collective-permute-start.17 = (f32[48,512]{1,0:T(8,128)S(1)}, f32[48,512]{1,0:T(8,128)S(1)}, u32[]{:S(2)}, u32[]{:S(2)}) collective-permute-start(f32[48,512]{1,0:T(8,128)S(1)} %maximum_select_fusion.4), channel_id=1, source_target_pairs={{0,8},{1,0},{2,10},{3,2},{4,12},{5,4},{6,14},{7,6},{8,9},{9,17},{1... | collective-permute-start | bytes 294920 | tf_op jit(solution)/shard_map/ppermute | solution.py:56
  70.1 8.9 %collective-permute-start.18 = (f32[48,512]{1,0:T(8,128)S(1)}, f32[48,512]{1,0:T(8,128)S(1)}, u32[]{:S(2)}, u32[]{:S(2)}) collective-permute-start(f32[48,512]{1,0:T(8,128)S(1)} %maximum_select_fusion.4), channel_id=1, source_target_pairs={{0,24},{1,16},{2,26},{3,18},{4,28},{5,20},{6,30},{7,22},{8,25},{9,... | collective-permute-start | bytes 294920 | tf_op jit(solution)/shard_map/ppermute | solution.py:56
  72.4 15.7 %collective-permute-start.7 = (f32[2,48,256]{2,1,0:T(8,128)S(1)}, f32[2,48,256]{2,1,0:T(8,128)S(1)}, u32[]{:S(2)}, u32[]{:S(2)}) collective-permute-start(f32[2,48,256]{2,1,0:T(8,128)S(1)} %fusion.15), channel_id=1, source_target_pairs={{0,1},{1,0},{2,3},{3,2},{4,5},{5,4},{6,7},{7,6},{8,9},{9,8},{10,11... | collective-permute-start | bytes 294920 | tf_op jit(solution)/shard_map/ppermute | solution.py:33
  74.3 15.9 %collective-permute-start.21 = (f32[2,48,512]{2,1,0:T(8,128)S(1)}, f32[2,48,512]{2,1,0:T(8,128)S(1)}, u32[]{:S(2)}, u32[]{:S(2)}) collective-permute-start(f32[2,48,512]{2,1,0:T(8,128)S(1)} %pad_maximum_fusion.1), channel_id=1, source_target_pairs={{0,4},{4,0},{8,12},{12,8},{16,20},{20,16},{24,28},{28,24},{1,5},{5... | collective-permute-start | bytes 589832 | tf_op jit(solution)/shard_map/ppermute | solution.py:63
  79.1 11.2 %collective-permute-start.24 = (f32[2,48,512]{2,1,0:T(8,128)S(1)}, f32[2,48,512]{2,1,0:T(8,128)S(1)}, u32[]{:S(2)}, u32[]{:S(2)}) collective-permute-start(f32[2,48,512]{2,1,0:T(8,128)S(1)} %pad_maximum_fusion.3), channel_id=1, source_target_pairs={{0,4},{4,0},{8,12},{12,8},{16,20},{20,16},{24,28},{28,24},{1,5},{5... | collective-permute-start | bytes 589832 | tf_op jit(solution)/shard_map/ppermute | solution.py:63
  83.2 16.0 %collective-permute-start.19 = (f32[48,1024]{1,0:T(8,128)S(1)}, f32[48,1024]{1,0:T(8,128)S(1)}, u32[]{:S(2)}, u32[]{:S(2)}) collective-permute-start(f32[48,1024]{1,0:T(8,128)S(1)} %fusion.5), channel_id=1, source_target_pairs={{0,2},{1,3},{2,0},{3,1},{4,6},{5,7},{6,4},{7,5},{8,10},{9,11},{10,... | collective-permute-start | bytes 589832 | tf_op jit(solution)/shard_map/ppermute | solution.py:33
  88.0 10.4 %collective-permute-start.14 = (f32[48,1024]{1,0:T(8,128)S(1)}, f32[48,1024]{1,0:T(8,128)S(1)}, u32[]{:S(2)}, u32[]{:S(2)}) collective-permute-start(f32[48,1024]{1,0:T(8,128)S(1)} %fusion.2), channel_id=1, source_target_pairs={{0,2},{1,3},{2,0},{3,1},{4,6},{5,7},{6,4},{7,5},{8,10},{9,11},{10,... | collective-permute-start | bytes 589832 | tf_op jit(solution)/shard_map/ppermute | solution.py:33
  93.3 10.5 %collective-permute-start.25 = (f32[48,1024]{1,0:T(8,128)S(1)}, f32[48,1024]{1,0:T(8,128)S(1)}, u32[]{:S(2)}, u32[]{:S(2)}) collective-permute-start(f32[48,1024]{1,0:T(8,128)S(1)} %fusion.11), channel_id=1, source_target_pairs={{0,2},{1,3},{2,0},{3,1},{4,6},{5,7},{6,4},{7,5},{8,10},{9,11},{10,... | collective-permute-start | bytes 589832 | tf_op jit(solution)/shard_map/ppermute | solution.py:33
  97.2 6.0 %collective-permute-start.22 = (f32[48,1024]{1,0:T(8,128)S(1)}, f32[48,1024]{1,0:T(8,128)S(1)}, u32[]{:S(2)}, u32[]{:S(2)}) collective-permute-start(f32[48,1024]{1,0:T(8,128)S(1)} %fusion.8), channel_id=1, source_target_pairs={{0,2},{1,3},{2,0},{3,1},{4,6},{5,7},{6,4},{7,5},{8,10},{9,11},{10,... | collective-permute-start | bytes 589832 | tf_op jit(solution)/shard_map/ppermute | solution.py:33
  (11 other events, 39.8 us)
